TPU v7x, 128 devices: a whole 4x4x4 slice. The times are simulated.
128 devices in a mesh: rows: 8 (over z, core), cols: 16 (over x, y).
Axes of the slice: x: 4, y: 4, z: 4, core: 2. Of those that a mesh axis runs over, the one named last changes fastest.
Arguments:
- embeddings: bfloat16 [917504, 1024], P(('rows', 'cols'))
- factor_cols: bfloat16 [917504, 512], P(('rows', 'cols')), may hold values from -0.12 to 0.12, as said below
- solved: int32 [917504], P(('rows', 'cols')), may hold values from 0 to 16
- pivots: int32 [256], replicated, may hold values from 0 to 917503, as said below
Outputs:
- new_cols: bfloat16 [917504, 256], P(('rows', 'cols'))
- gains: float32 [917504], P(('rows', 'cols'))
- best_gain: float32 [], replicated
Inputs may be any that keep to these rules, and one draw needn't show every extreme that they name: `pivots`: 256 distinct row numbers in increasing order; the 7168 consecutive rows of one device hold at most 16 of them, and some device holds exactly 16. `factor_cols`: the pivots' factor rows F satisfy: every eigenvalue of F F^T is below 1.
All inputs are finite; a program needn't handle non-finite values.
Results may differ from a plain program's by a relative error of at most 0.001.
Values may be sent and summed in bfloat16 or wider, within the bound.
No kernel may reach another device: no remote copies, remote signals or barrier semaphores. Data moves between devices by JAX's collectives and lax.ppermute only.
A program may use at most 128 MiB of HBM per device.

v0:
```python
import jax
import jax.numpy as jnp
from jax import lax
from jax.sharding import PartitionSpec as P

PMAX = 16
EPS = 1e-06
TAU = 6.0
RIDGE = 1.0


def learn(counts):
    c = counts.astype(jnp.float32)
    return (c * (16.0 - c) + 8.0) / 72.0


def scales(emb):
    x = emb.astype(jnp.float32)
    return jnp.sqrt(jnp.mean(x * x, axis=1) + EPS)


def kernel_panel(
    left_emb, left_fac, left_q, left_norm, left_ids, piv_emb, piv_fac, piv_q, piv_norm, pivots
):
    dims = (((1,), (1,)), ((), ()))
    dots = lax.dot_general(left_emb, piv_emb, dims, preferred_element_type=jnp.float32)
    width = left_emb.shape[1] * 1.0
    cosine = dots / (width * left_norm[:, None] * piv_norm[None, :])
    similar = jnp.exp(TAU * (cosine - 1.0))
    ridge = jnp.where(left_ids[:, None] == pivots[None, :], RIDGE, 0.0)
    shared = lax.dot_general(left_fac, piv_fac, dims, preferred_element_type=jnp.float32)
    return left_q[:, None] * piv_q[None, :] * similar + ridge - shared


def body(embeddings, factor_cols, solved, pivots):
    rows_here = embeddings.shape[0]
    total = pivots.shape[0]
    device = lax.axis_index(("rows", "cols"))
    first_row = device * rows_here
    owner = pivots // rows_here
    before = jnp.sum((owner < device).astype(jnp.int32))
    mine = jnp.sum((owner == device).astype(jnp.int32))
    ranks = jnp.arange(PMAX, dtype=jnp.int32)
    valid = ranks < mine
    position = jnp.clip(before + ranks, 0, total - 1)
    local_idx = jnp.clip(pivots[position] - first_row, 0, rows_here - 1)
    keep = valid[:, None]
    own_emb = jnp.where(keep, embeddings[local_idx], 0)
    own_fac = jnp.where(keep, factor_cols[local_idx], 0)
    own_count = jnp.where(valid, solved[local_idx], 0).astype(jnp.bfloat16)
    place = (
        (jnp.arange(total, dtype=jnp.int32)[:, None] == (before + ranks)[None, :]) & valid[None, :]
    ).astype(jnp.float32)
    highest = lax.Precision.HIGHEST
    all_emb, all_fac, all_count = (
        lax.all_gather(own_emb, ("rows", "cols"), axis=0, tiled=True),
        lax.all_gather(own_fac, ("rows", "cols"), axis=0, tiled=True),
        lax.all_gather(own_count, ("rows", "cols"), axis=0, tiled=True),
    )
    earlier = jnp.sum((owner[None, :] < owner[:, None]).astype(jnp.int32), axis=1)
    slot_index = owner * PMAX + jnp.arange(total, dtype=jnp.int32) - earlier
    piv_emb = all_emb[slot_index]
    piv_fac = all_fac[slot_index]
    piv_count = all_count[slot_index].astype(jnp.float32)
    row_q = learn(solved)
    piv_q = learn(piv_count)
    piv_norm = scales(piv_emb)
    row_ids = first_row + jnp.arange(rows_here, dtype=jnp.int32)
    panel = kernel_panel(
        embeddings,
        factor_cols,
        row_q,
        scales(embeddings),
        row_ids,
        piv_emb,
        piv_fac,
        piv_q,
        piv_norm,
        pivots,
    )
    own_rows = jnp.where(keep, panel[local_idx], 0.0)
    block = lax.psum(jnp.dot(place, own_rows, precision=highest), ("rows", "cols"))
    lower = jnp.linalg.cholesky(block)
    full = jax.scipy.linalg.solve_triangular(lower, panel.T, lower=True).T
    facf = factor_cols.astype(jnp.float32)
    gains = row_q * row_q + RIDGE - jnp.sum(facf * facf, axis=1) - jnp.sum(full * full, axis=1)
    best = lax.pmax(jnp.max(gains), ("rows", "cols"))
    return (full.astype(jnp.bfloat16), gains, best)


def solution(mesh):
    in_specs = (P(("rows", "cols"), None), P(("rows", "cols"), None), P(("rows", "cols")), P())
    out_specs = (P(("rows", "cols"), None), P(("rows", "cols")), P())
    return jax.shard_map(body, mesh=mesh, in_specs=in_specs, out_specs=out_specs, check_vma=False)
```

profile of v0, /device:TPU:1, one launch (start us, length us, event | category | flops | bytes accessed | tf_op | source)
XLA Modules:
  0.0 518.1 jit_solution(16837783540909877693)
XLA Ops:
  11.2 4.6 gather_fusion.5
  16.6 7.7 %gather_fusion.3 = bf16[16,1024]{1,0:T(8,128)(2,1)S(1)} fusion(bf16[7168,1024]{1,0:T(8,128)(2,1)} %param.4, s32[1024]{0:T(1024)S(1)} %pad_clamp_fusion.1), kind=kCustom, calls=%fused_computation.3 | custom fusion | bytes 65600 | tf_op jit(solution)/shard_map/gather | solution.py:48
  27.3 69.2 %all-reduce.1 = bf16[2048]{0:T(1024)(128)(2,1)S(1)} all-reduce(bf16[2048]{0:T(1024)(128)(2,1)S(1)} %dynamic-update-slice.11), channel_id=1, replica_groups=mesh['rows'=8,'cols'=16] {'rows','cols'}, use_global_device_ids=true, to_apply=%add.1 | all-reduce | flops 2048 | bytes 8192
  99.3 8.1 %multiply_reduce_fusion = f32[7168]{0:T(1024)S(1)} fusion(bf16[7168,1024]{1,0:T(8,128)(2,1)} %param.4), kind=kLoop, calls=%fused_computation.10 | loop fusion | flops 22012928 | bytes 14708736 | tf_op jit(solution)/shard_map/reduce_sum | solution.py:19
  107.5 3.1 gather_fusion.6
  110.6 42.8 %all-gather.3.cloned.1.call-done = bf16[2048,1024]{1,0:T(8,128)(2,1)} async-done(((bf16[16,1024]{1,0:T(8,128)(2,1)}), bf16[2048,1024]{1,0:T(8,128)(2,1)}) %all-gather.3.cloned.1.call-update) | async-done | bytes 4194320 | tf_op jit(solution)/shard_map/all_gather | solution.py:56
  153.4 4.3 gather_fusion.4
  157.7 16.8 %fusion.34 = f32[256,7168]{1,0:T(8,128)} fusion(bf16[256,1024]{1,0:T(8,128)(2,1)S(1)} %gather_fusion.4, bf16[7168,1024]{1,0:T(8,128)(2,1)} %param.4), kind=kOutput, calls=%fused_computation.90 | convolution fusion | flops 3758096384 | bytes 22544384 | tf_op jit(solution)/shard_map/dot_general | solution.py:26
  174.7 25.6 %add_subtract_fusion = (f32[256,7168]{1,0:T(8,128)}, f32[256,7168]{1,0:T(8,128)}) fusion(f32[256,7168]{1,0:T(8,128)} %fusion.34, s32[7168]{0:T(1024)S(1)} %iota_add_fusion, f32[256]{0:T(256)S(1)} %add_sqrt_fusion, f32[7168]{0:T(1024)S(1)} %get-tuple-element.44, f32[256]{0:T(256)S(1)} %fusion.26, f32[7168]{0:T(1024)S(1)} %get-tuple-element.43, ...), kind=kOutput, calls=%fused_computation.22 | convolution fusion | flops 1897398272 | bytes 29711360 | tf_op jit(solution)/shard_map/dot_general | solution.py:31
  200.3 7.2 %bitcast_subtract_fusion = f32[7168,256]{0,1:T(8,128)} fusion(f32[256,7168]{1,0:T(8,128)} %get-tuple-element.40, f32[256,7168]{1,0:T(8,128)S(1)} %bitcast.60, s32[7168]{0:T(1024)S(1)} %iota_add_fusion, f32[256]{0:T(256)S(1)} %add_sqrt_fusion, f32[7168]{0:T(1024)S(1)} %get-tuple-element.44, f32[256]{0:T(256)S(1)} %fusion.26, f32[7168]{0:T(1024)S(1)} %get-tuple-element.43, ...), kind=kLoop, calls=%fused_computation.14 | loop fusion | flops 18350080 | bytes 22109184 | tf_op jit(solution)/shard_map/sub | solution.py:32
  207.6 8.4 %copy.15 = f32[7168,256]{1,0:T(8,128)} copy(f32[7168,256]{0,1:T(8,128)} %bitcast_subtract_fusion) | data formatting | bytes 14680064 | tf_op jit(solution)/shard_map/sub | solution.py:32
  215.9 3.7 gather_fusion.7
  220.7 4.6 multiply_reduce_fusion.1
  225.3 135.9 %all-reduce.4.cloned.1.call-done = f32[256,256]{0,1:T(8,128)} async-done(((f32[256,256]{0,1:T(8,128)}), f32[256,256]{0,1:T(8,128)}) %all-reduce.4.cloned.1.call-update) | async-done | bytes 262160 | tf_op jit(solution)/shard_map/psum | solution.py:82
  363.3 11.7 %cholesky.50 = f32[128,128]{1,0:T(8,128)S(1)} custom-call(f32[128,128]{1,0:T(8,128)S(1)} %cholesky.118), custom_call_target="Cholesky" | custom-call | tf_op jit(solution)/shard_map/jit(cholesky)/cholesky | solution.py:83
  375.1 9.8 %custom-call.15 = f32[1,128,128]{1,2,0:T(8,128)S(1)} custom-call(f32[1,128,128]{2,1,0:T(8,128)S(1)} %get-tuple-element.38), custom_call_target="InvertDiagBlocksLowerTriangular" | custom-call | tf_op jit(solution)/shard_map/jit(cholesky)/cholesky | solution.py:83
  385.4 11.7 %cholesky.105 = f32[128,128]{1,0:T(8,128)S(1)} custom-call(f32[128,128]{1,0:T(8,128)S(1)} %convolution_subtract_fusion.1), custom_call_target="Cholesky" | custom-call | tf_op jit(solution)/shard_map/jit(cholesky)/cholesky | solution.py:83
  399.8 4.0 while.1
  403.8 19.9 %custom-call.16 = f32[2,128,128]{1,2,0:T(8,128)S(1)} custom-call(f32[2,128,128]{2,1,0:T(8,128)S(1)} %get-tuple-element.10), custom_call_target="InvertDiagBlocksLowerTriangular" | custom-call | tf_op jit(solution)/shard_map/jit(_solve_triangular)/triangular_solve | solution.py:84
  423.7 5.5 %fusion.7 = f32[128,7168]{1,0:T(8,128)S(1)} fusion(f32[256,7168]{1,0:T(8,128)} %get-tuple-element.39, f32[2,128,128]{1,2,0:T(8,128)S(1)} %custom-call.16), kind=kOutput, calls=%fused_computation.25 | convolution fusion | flops 1409286144 | bytes 7405568 | tf_op jit(solution)/shard_map/jit(_solve_triangular)/triangular_solve | solution.py:84
  429.2 5.3 %convolution_subtract_fusion = f32[128,7168]{1,0:T(8,128)S(1)} fusion(f32[128,7168]{1,0:T(8,128)S(1)} %fusion.7, f32[256,7168]{1,0:T(8,128)} %get-tuple-element.39, f32[256,256]{1,0:T(8,128)S(1)} %get-tuple-element.94), kind=kOutput, calls=%fused_computation.12 | convolution fusion | flops 1410203648 | bytes 11075584 | tf_op jit(solution)/shard_map/jit(_solve_triangular)/triangular_solve | solution.py:84
  434.5 3.5 fusion.14
  442.1 63.3 %pmax.7 = f32[]{:T(128)} all-reduce(f32[]{:T(128)} %get-tuple-element.30), channel_id=1, replica_groups=mesh['rows'=8,'cols'=16] {'rows','cols'}, use_global_device_ids=true, to_apply=%region_13.14 | all-reduce | flops 1 | bytes 8 | tf_op jit(solution)/shard_map/pmax | solution.py:87
  505.4 5.9 %copy.18 = bf16[7168,256]{1,0:T(8,128)(2,1)} copy(bf16[7168,256]{0,1:T(8,128)(2,1)} %fusion.6) | data formatting | bytes 7340032
  (63 shorter events, 24.0 us)
Async XLA Ops:
  7.2 100.4 %all-gather.5.cloned.1.call-start = ((), (), s32[]{:S(2)}) async-start(), calls=%async_computation.1 | async-start | bytes 2113536 | tf_op jit(solution)/shard_map/all_gather | solution.py:57
  16.5 136.8 %all-gather.3.cloned.1.call-start = ((), (), s32[]{:S(2)}) async-start(), calls=%async_computation | async-start | bytes 4227072 | tf_op jit(solution)/shard_map/all_gather | solution.py:56
  25.0 336.2 %all-reduce.4.cloned.1.call-start = ((), (), s32[]{:S(2)}) async-start(), calls=%async_computation.2 | async-start | bytes 524288 | tf_op jit(solution)/shard_map/psum | solution.py:82
  99.3 8.1 %copy-start.1 = (s32[7168]{0:T(1024)S(1)}, s32[7168]{0:T(1024)}, u32[]{:S(2)}) copy-start(s32[7168]{0:T(1024)} %param.6) | copy-start | bytes 86020
  157.7 17.0 %copy-start = (s32[256]{0:T(256)S(1)}, s32[256]{0:T(256)}, u32[]{:S(2)}) copy-start(s32[256]{0:T(256)} %param.7) | copy-start | bytes 3076
  174.5 25.9 %slice-start = ((s8[7340032]{0:T(1024)(128)(4,1)}), s8[4194304]{0:T(1024)(128)(4,1)S(1)}, s32[]{:S(2)}) async-start(s8[7340032]{0:T(1024)(128)(4,1)} %bitcast.59), calls=%async_computation.3 | async-start | bytes 8388608
  174.7 25.7 %slice-start.1 = ((s8[7340032]{0:T(1024)(128)(4,1)}), s8[3145728]{0:T(1024)(128)(4,1)S(1)}, s32[]{:S(2)}) async-start(s8[7340032]{0:T(1024)(128)(4,1)} %bitcast.59), calls=%async_computation.4 | async-start | bytes 6291456
Sparse Core Ops, SparseCore 0:
  16.6 69.0 all-gather.4
  89.4 63.9 all-gather.2
  220.8 140.3 all-reduce.3
where the time goes:
time: 522 us; the launch traced here: 518 us
  waiting for transfers between devices  179 us (34%)
  blocking collectives  133 us (25%)
  other arithmetic  85.1 us (16%)
  matrix products  58.3 us (11%)
  local copies, waits for them, and re-layouts  47.7 us (9%)
  between operations  15.6 us (3%)
    psum x1, waiting for transfers between devices, body(): lax.psum(jnp.dot(place, own_rows, precision=highest), ('rows', 'cols'))  136 us
    unnamed x1, blocking collectives  69.2 us
    pmax x1, blocking collectives, body(): best = lax.pmax(jnp.max(gains), ('rows', 'cols'))  63.3 us
    all_gather x1, waiting for transfers between devices, body(): lax.all_gather(own_emb, ('rows', 'cols'), axis=0, tiled=True)  42.8 us
    another operation x7, other arithmetic, body(): lower = jnp.linalg.cholesky(block)  34.6 us
    dot_general x1, matrix products, kernel_panel(): lax.dot_general(left_fac, piv_fac, dims, preferred_element_type=jnp.float32)  25.6 us
    another operation x3, other arithmetic, body(): full = jax.scipy.linalg.solve_triangular(lower, panel.T, lower=True).T  19.9 us
    dot_general x1, matrix products, kernel_panel(): lax.dot_general(left_emb, piv_emb, dims, preferred_element_type=jnp.float32)  16.8 us
  transfers between devices with their start and end apart: 3, of which 2 were waited for; matrix products, arithmetic and copies ran while one was open for 6% of the time, Pallas kernels for 0%

commit v1 on v0

--- a/solution.py
+++ b/solution.py
@@ -2,6 +2,7 @@
 import jax.numpy as jnp
 from jax import lax
 from jax.sharding import PartitionSpec as P
+from jax.lax import all_gather
 
 PMAX = 16
 EPS = 1e-06
@@ -79,7 +80,8 @@
         pivots,
     )
     own_rows = jnp.where(keep, panel[local_idx], 0.0)
-    block = lax.psum(jnp.dot(place, own_rows, precision=highest), ("rows", "cols"))
+    z = jnp.dot(place, own_rows, precision=highest)
+    block = jnp.sum(all_gather(z, ("rows", "cols")), 0)
     lower = jnp.linalg.cholesky(block)
     full = jax.scipy.linalg.solve_triangular(lower, panel.T, lower=True).T
     facf = factor_cols.astype(jnp.float32)

time: 522 us -> 486 us (0.931)
  waiting for transfers between devices: 179 us -> 142 us
  matrix products: 58.3 us -> 46.5 us
  other arithmetic: 85.1 us -> 96.4 us
    psum x1 -> x0, waiting for transfers between devices: 136 us -> none  [body(): lax.psum(jnp.dot(place, own_rows, precision=highest), ('rows', 'cols'))]
    all_gather x0 -> x1, waiting for transfers between devices: none -> 99.5 us  [body(): block = jnp.sum(all_gather(z, ('rows', 'cols')), 0)]
    dot_general x1, matrix products: 25.6 us -> 13.5 us  [kernel_panel(): lax.dot_general(left_fac, piv_fac, dims, preferred_element_type=jnp.float32)]
    reduce_sum x0 -> x1, other arithmetic: none -> 12.1 us  [body(): block = jnp.sum(all_gather(z, ('rows', 'cols')), 0)]
where the time goes in v1:
time: 486 us; the launch traced here: 481 us
  waiting for transfers between devices  142 us (29%)
  blocking collectives  134 us (28%)
  other arithmetic  96.4 us (20%)
  local copies, waits for them, and re-layouts  46.7 us (10%)
  matrix products  46.5 us (10%)
  between operations  15.6 us (3%)
    all_gather x1, waiting for transfers between devices, body(): block = jnp.sum(all_gather(z, ('rows', 'cols')), 0)  99.5 us
    unnamed x1, blocking collectives  69.1 us
    pmax x1, blocking collectives, body(): best = lax.pmax(jnp.max(gains), ('rows', 'cols'))  64.5 us
    all_gather x1, waiting for transfers between devices, body(): lax.all_gather(own_emb, ('rows', 'cols'), axis=0, tiled=True)  42.9 us
    another operation x7, other arithmetic, body(): lower = jnp.linalg.cholesky(block)  34.6 us
    another operation x3, other arithmetic, body(): full = jax.scipy.linalg.solve_triangular(lower, panel.T, lower=True).T  19.9 us
    dot_general x1, matrix products, kernel_panel(): lax.dot_general(left_emb, piv_emb, dims, preferred_element_type=jnp.float32)  16.9 us
    another operation x3, matrix products, body(): full = jax.scipy.linalg.solve_triangular(lower, panel.T, lower=True).T  14.6 us
  transfers between devices with their start and end apart: 3, of which 2 were waited for; matrix products, arithmetic and copies ran while one was open for 6% of the time, Pallas kernels for 0%

profile of v1, /device:TPU:1, one launch (start us, length us, event | category | flops | bytes accessed | tf_op | source)
XLA Modules:
  0.0 481.4 jit_solution(9502996314257893807)
XLA Ops:
  11.2 4.6 gather_fusion.5
  16.6 7.7 %gather_fusion.3 = bf16[16,1024]{1,0:T(8,128)(2,1)S(1)} fusion(bf16[7168,1024]{1,0:T(8,128)(2,1)} %param.4, s32[1024]{0:T(1024)S(1)} %pad_clamp_fusion.1), kind=kCustom, calls=%fused_computation.3 | custom fusion | bytes 65600 | tf_op jit(solution)/shard_map/gather | solution.py:49
  27.3 69.1 %all-reduce.1 = bf16[2048]{0:T(1024)(128)(2,1)S(1)} all-reduce(bf16[2048]{0:T(1024)(128)(2,1)S(1)} %dynamic-update-slice.11), channel_id=1, replica_groups=mesh['rows'=8,'cols'=16] {'rows','cols'}, use_global_device_ids=true, to_apply=%add.1 | all-reduce | flops 2048 | bytes 8192
  99.2 8.1 %multiply_reduce_fusion = f32[7168]{0:T(1024)S(1)} fusion(bf16[7168,1024]{1,0:T(8,128)(2,1)} %param.4), kind=kLoop, calls=%fused_computation.10 | loop fusion | flops 22012928 | bytes 14708736 | tf_op jit(solution)/shard_map/reduce_sum | solution.py:20
  110.5 42.9 %all-gather.5.cloned.1.call-done = bf16[2048,1024]{1,0:T(8,128)(2,1)} async-done(((bf16[16,1024]{1,0:T(8,128)(2,1)}), bf16[2048,1024]{1,0:T(8,128)(2,1)}) %all-gather.5.cloned.1.call-update) | async-done | bytes 4194320 | tf_op jit(solution)/shard_map/all_gather | solution.py:57
  153.4 4.3 gather_fusion.4
  157.7 16.9 %fusion.34 = f32[256,7168]{1,0:T(8,128)} fusion(bf16[256,1024]{1,0:T(8,128)(2,1)S(1)} %gather_fusion.4, bf16[7168,1024]{1,0:T(8,128)(2,1)} %param.4), kind=kOutput, calls=%fused_computation.90 | convolution fusion | flops 3758096384 | bytes 22544384 | tf_op jit(solution)/shard_map/dot_general | solution.py:27
  174.8 13.5 %add_subtract_fusion = (f32[256,7168]{1,0:T(8,128)}, f32[256,7168]{1,0:T(8,128)}) fusion(f32[256,7168]{1,0:T(8,128)} %fusion.34, s32[7168]{0:T(1024)S(1)} %iota_add_fusion, f32[256]{0:T(256)S(1)} %add_sqrt_fusion, f32[7168]{0:T(1024)S(1)} %get-tuple-element.47, f32[256]{0:T(256)S(1)} %fusion.26, f32[7168]{0:T(1024)S(1)} %get-tuple-element.46, ...), kind=kOutput, calls=%fused_computation.22 | convolution fusion | flops 1897398272 | bytes 29711360 | tf_op jit(solution)/shard_map/dot_general | solution.py:32
  188.3 7.3 %bitcast_subtract_fusion = f32[7168,256]{0,1:T(8,128)} fusion(f32[256,7168]{1,0:T(8,128)} %get-tuple-element.43, f32[256,7168]{1,0:T(8,128)S(1)} %bitcast.62, s32[7168]{0:T(1024)S(1)} %iota_add_fusion, f32[256]{0:T(256)S(1)} %add_sqrt_fusion, f32[7168]{0:T(1024)S(1)} %get-tuple-element.47, f32[256]{0:T(256)S(1)} %fusion.26, f32[7168]{0:T(1024)S(1)} %get-tuple-element.46, ...), kind=kLoop, calls=%fused_computation.14 | loop fusion | flops 18350080 | bytes 22109184 | tf_op jit(solution)/shard_map/sub | solution.py:33
  195.6 8.4 %copy.16 = f32[7168,256]{1,0:T(8,128)} copy(f32[7168,256]{0,1:T(8,128)} %bitcast_subtract_fusion) | data formatting | bytes 14680064 | tf_op jit(solution)/shard_map/sub | solution.py:33
  204.0 3.7 gather_fusion.7
  208.7 4.6 multiply_reduce_fusion.1
  213.3 99.5 %all-gather.9.cloned.1.call-done = f32[32768,256]{1,0:T(8,128)} async-done(((f32[256,256]{1,0:T(8,128)}), f32[32768,256]{1,0:T(8,128)}) %all-gather.9.cloned.1.call-update) | async-done | bytes 33554448 | tf_op jit(solution)/shard_map/all_gather | solution.py:84
  312.8 12.1 %reduce_sum.77 = f32[256,256]{1,0:T(8,128)S(1)} reduce(f32[128,256,256]{2,1,0:T(8,128)} %bitcast.60, f32[]{:T(128)} %constant.136.clone.1), dimensions={0}, to_apply=%region_5.6 | reduce | flops 8323072 | bytes 33816580 | tf_op jit(solution)/shard_map/reduce_sum | solution.py:84
  325.1 11.7 %cholesky.50 = f32[128,128]{1,0:T(8,128)S(1)} custom-call(f32[128,128]{1,0:T(8,128)S(1)} %cholesky.118), custom_call_target="Cholesky" | custom-call | tf_op jit(solution)/shard_map/jit(cholesky)/cholesky | solution.py:85
  336.9 9.8 %custom-call.15 = f32[1,128,128]{1,2,0:T(8,128)S(1)} custom-call(f32[1,128,128]{2,1,0:T(8,128)S(1)} %get-tuple-element.41), custom_call_target="InvertDiagBlocksLowerTriangular" | custom-call | tf_op jit(solution)/shard_map/jit(cholesky)/cholesky | solution.py:85
  347.2 11.7 %cholesky.105 = f32[128,128]{1,0:T(8,128)S(1)} custom-call(f32[128,128]{1,0:T(8,128)S(1)} %convolution_subtract_fusion.1), custom_call_target="Cholesky" | custom-call | tf_op jit(solution)/shard_map/jit(cholesky)/cholesky | solution.py:85
  361.6 4.0 while.1
  365.6 19.9 %custom-call.16 = f32[2,128,128]{1,2,0:T(8,128)S(1)} custom-call(f32[2,128,128]{2,1,0:T(8,128)S(1)} %get-tuple-element.10), custom_call_target="InvertDiagBlocksLowerTriangular" | custom-call | tf_op jit(solution)/shard_map/jit(_solve_triangular)/triangular_solve | solution.py:86
  385.5 5.5 %fusion.7 = f32[128,7168]{1,0:T(8,128)S(1)} fusion(f32[256,7168]{1,0:T(8,128)} %get-tuple-element.42, f32[2,128,128]{1,2,0:T(8,128)S(1)} %custom-call.16), kind=kOutput, calls=%fused_computation.25 | convolution fusion | flops 1409286144 | bytes 7405568 | tf_op jit(solution)/shard_map/jit(_solve_triangular)/triangular_solve | solution.py:86
  391.0 5.6 %convolution_subtract_fusion = f32[128,7168]{1,0:T(8,128)S(1)} fusion(f32[128,7168]{1,0:T(8,128)S(1)} %fusion.7, f32[256,7168]{1,0:T(8,128)} %get-tuple-element.42, f32[256,256]{1,0:T(8,128)S(1)} %get-tuple-element.98), kind=kOutput, calls=%fused_computation.12 | convolution fusion | flops 1410203648 | bytes 11075584 | tf_op jit(solution)/shard_map/jit(_solve_triangular)/triangular_solve | solution.py:86
  396.6 3.5 fusion.14
  404.3 64.5 %pmax.7 = f32[]{:T(128)} all-reduce(f32[]{:T(128)} %get-tuple-element.33), channel_id=1, replica_groups=mesh['rows'=8,'cols'=16] {'rows','cols'}, use_global_device_ids=true, to_apply=%region_13.14 | all-reduce | flops 1 | bytes 8 | tf_op jit(solution)/shard_map/pmax | solution.py:89
  468.7 5.9 %copy.18 = bf16[7168,256]{1,0:T(8,128)(2,1)} copy(bf16[7168,256]{0,1:T(8,128)(2,1)} %fusion.6) | data formatting | bytes 7340032
  (64 shorter events, 25.0 us)
Async XLA Ops:
  7.2 100.3 %all-gather.7.cloned.1.call-start = ((), (), s32[]{:S(2)}) async-start(), calls=%async_computation.1 | async-start | bytes 2113536 | tf_op jit(solution)/shard_map/all_gather | solution.py:58
  16.5 136.9 %all-gather.5.cloned.1.call-start = ((), (), s32[]{:S(2)}) async-start(), calls=%async_computation | async-start | bytes 4227072 | tf_op jit(solution)/shard_map/all_gather | solution.py:57
  25.0 287.8 %all-gather.9.cloned.1.call-start = ((), (), s32[]{:S(2)}) async-start(), calls=%async_computation.2 | async-start | bytes 33816576 | tf_op jit(solution)/shard_map/all_gather | solution.py:84
  99.2 8.1 %copy-start.1 = (s32[7168]{0:T(1024)S(1)}, s32[7168]{0:T(1024)}, u32[]{:S(2)}) copy-start(s32[7168]{0:T(1024)} %param.6) | copy-start | bytes 86020
  157.7 17.1 %copy-start = (s32[256]{0:T(256)S(1)}, s32[256]{0:T(256)}, u32[]{:S(2)}) copy-start(s32[256]{0:T(256)} %param.7) | copy-start | bytes 3076
  174.5 13.7 %slice-start = ((s8[7340032]{0:T(1024)(128)(4,1)}), s8[4194304]{0:T(1024)(128)(4,1)S(1)}, s32[]{:S(2)}) async-start(s8[7340032]{0:T(1024)(128)(4,1)} %bitcast.61), calls=%async_computation.3 | async-start | bytes 8388608
  174.7 13.5 %slice-start.1 = ((s8[7340032]{0:T(1024)(128)(4,1)}), s8[3145728]{0:T(1024)(128)(4,1)S(1)}, s32[]{:S(2)}) async-start(s8[7340032]{0:T(1024)(128)(4,1)} %bitcast.61), calls=%async_computation.4 | async-start | bytes 6291456
Sparse Core Ops, SparseCore 0:
  16.6 69.0 all-gather.6
  89.4 63.9 all-gather.4
  208.8 103.9 all-gather.8
